TPU v7x, 256 devices: a whole 4x4x8 slice. The times are simulated.
256 devices in a mesh: wide: 32 (over z_lo, y, core), narrow: 8 (over z_hi, x).
Axes of the slice: x: 4, y: 4, z: 8 (z_hi: 2, z_lo: 4; z = z_hi * 4 + z_lo), core: 2. Of those that a mesh axis runs over, the one named last changes fastest.
Arguments:
- gradient: float32 [3072, 3072], P('wide', 'narrow'), may hold values from -6 to 6
- first_moment: float32 [3072, 3072], P('wide', 'narrow'), may hold values from -6 to 6
- second_moment: float32 [3072, 3072], P('wide', 'narrow'), may hold values from 0.25 to 4
- left_basis: float32 [3072, 3072], P('wide', 'narrow'), may hold values from -0.21875 to 0.21875
- right_basis: float32 [3072, 3072], P('wide', 'narrow'), may hold values from -0.109375 to 0.109375
Outputs:
- update: float32 [3072, 3072], P('wide', 'narrow')
- new_first: float32 [3072, 3072], P('wide', 'narrow')
- new_second: float32 [3072, 3072], P('wide', 'narrow')
All inputs are finite; a program needn't handle non-finite values.
Results may differ from a plain program's by a relative error of at most 0.000075.
Values sent between devices are 32-bit elements; how exact they have to be, the bound alone decides.
No kernel may reach another device: no remote copies, remote signals or barrier semaphores. Data moves between devices by JAX's collectives and lax.ppermute only.
A program may use at most 64 MiB of HBM per device.

v0:
```python
import jax
import jax.numpy as jnp
from jax import lax
from jax.sharding import Mesh
from jax.sharding import PartitionSpec as P

STEP = 10
WIDE = ("wide_0", "wide_1", "wide_2")
beta_first = 0.9
beta_second = 0.95
epsilon = 1e-08


def side_by_side(arrays, axis, dim, along):
    ends, at = ([], 0)
    for a in arrays[:-1]:
        at += a.shape[along]
        ends.append(at)
    both = jnp.concatenate(arrays, axis=along)
    return tuple(jnp.split(lax.all_gather(both, axis, axis=dim, tiled=True), ends, axis=along))


def in_blocks(value, dim, peers):
    lengths = value.shape
    tiles = value.reshape(*lengths[:dim], peers, lengths[dim] // peers, *lengths[dim + 1 :])
    return jnp.moveaxis(tiles, dim, 0)


def scatter_pairs(value, chips, core, dim):
    sizes = (lax.axis_size(chips), lax.axis_size(core))
    tiles = in_blocks(value, dim, sizes[0] * sizes[1])
    inside = tiles.shape[1:]
    tiles = tiles.reshape(*sizes, *inside).swapaxes(0, 1).reshape(-1, *inside)
    tiles = lax.psum_scatter(tiles, core, scatter_dimension=0, tiled=True)
    return lax.psum_scatter(tiles, chips, scatter_dimension=0, tiled=True)[0]


def sent_and_summed(value, axis, dim):
    tiles = in_blocks(value, dim, lax.axis_size(axis))
    arrived = lax.all_to_all(tiles, axis, split_axis=0, concat_axis=0, tiled=True)
    return arrived.sum(axis=0)


def product(left, right):
    return jnp.dot(left, right, precision=lax.Precision.HIGHEST, preferred_element_type=jnp.float32)


def contract(left, right, left_dim, right_dim):
    return lax.dot_general(
        left,
        right,
        (((left_dim,), (right_dim,)), ((), ())),
        precision=lax.Precision.HIGHEST,
        preferred_element_type=jnp.float32,
    )


def body(gradient, first_moment, second_moment, left_basis, right_basis):
    grad_rows, left_rows = side_by_side((gradient, left_basis), "narrow", 1, 0)
    right_panel = lax.all_gather(right_basis, WIDE, axis=0, tiled=True)
    rotated_right = product(grad_rows, right_panel)
    columns = left_rows
    rotated = scatter_pairs(
        contract(columns, rotated_right, 0, 0), ("wide_0", "wide_1"), "wide_2", 0
    )
    new_first = beta_first * first_moment + (1.0 - beta_first) * rotated
    new_second = beta_second * second_moment + (1.0 - beta_second) * rotated * rotated
    direction = (
        new_first
        / (1.0 - beta_first**STEP)
        / (jnp.sqrt(new_second / (1.0 - beta_second**STEP)) + epsilon)
    )
    columns = left_rows
    back_left = product(columns, lax.all_gather(direction, WIDE, axis=0, tiled=True))
    terms = contract(back_left, right_panel, 1, 1)
    update = sent_and_summed(terms, "narrow", 1)
    return (update, new_first, new_second)


def solution(mesh):
    torus = Mesh(
        mesh.devices.reshape(4, 4, 2, mesh.shape["narrow"]),
        ("wide_0", "wide_1", "wide_2", "narrow"),
    )
    return jax.shard_map(
        body,
        mesh=torus,
        in_specs=(
            P(WIDE, "narrow"),
            P(WIDE, "narrow"),
            P(WIDE, "narrow"),
            P(WIDE, "narrow"),
            P(WIDE, "narrow"),
        ),
        out_specs=(P(WIDE, "narrow"), P(WIDE, "narrow"), P(WIDE, "narrow")),
        check_vma=False,
    )
```

profile of v0, /device:TPU:32, one launch (start us, length us, event | category | flops | bytes accessed | tf_op | source)
XLA Modules:
  0.0 398.6 jit_solution(4710670992428549391)
XLA Ops:
  7.2 0.0 all-gather.4.cloned.1.call-start
  7.2 1.7 pad_maximum_fusion
  8.9 0.0 all-gather.4.cloned.1.call-update
  9.0 0.0 all-gather.6.cloned.1.call-start
  9.0 0.7 all-gather.6.cloned.1.call-update
  9.7 0.0 reduce-scatter.3.cloned.1.call-start
  9.8 82.1 %all-gather.4.cloned.1.call-done = f32[192,3072]{1,0:T(8,128)} async-done(((f32[192,384]{1,0:T(8,128)}), f32[192,3072]{1,0:T(8,128)}) %all-gather.4.cloned.1.call-update) | async-done | bytes 2359312 | tf_op jit(solution)/shard_map/all_gather | solution.py:20
  91.8 62.0 %all-gather.6.cloned.1.call-done = f32[3072,384]{1,0:T(8,128)} async-done(((f32[96,384]{1,0:T(8,128)}), f32[3072,384]{1,0:T(8,128)}) %all-gather.6.cloned.1.call-update) | async-done | bytes 4718608 | tf_op jit(solution)/shard_map/all_gather | solution.py:60
  153.8 5.6 %fusion = f32[96,384]{1,0:T(8,128)S(1)} fusion(f32[3072,384]{1,0:T(8,128)} %all-gather.6.cloned.1.call-done, f32[192,3072]{1,0:T(8,128)} %all-gather.4.cloned.1.call-done), kind=kOutput, calls=%fused_computation.1 | convolution fusion | flops 1358954496 | bytes 6045696 | tf_op jit(solution)/shard_map/dot_general | solution.py:45
  159.4 3.9 fusion.4
  163.3 2.5 copy.9
  165.9 0.0 reduce-scatter.3.cloned.1.call-update
  165.9 0.0 reduce-scatter.5.cloned.1.call-start
  166.0 17.3 %reduce-scatter.3.cloned.1.call-done = f32[16,96,384]{2,1,0:T(8,128)} async-done(((f32[32,96,384]{2,1,0:T(8,128)}), f32[16,96,384]{2,1,0:T(8,128)}) %reduce-scatter.3.cloned.1.call-update) | async-done | bytes 2359312 | tf_op jit(solution)/shard_map/reduce_scatter | solution.py:34
  183.3 0.0 reduce-scatter.5.cloned.1.call-update
  183.3 0.2 all-gather.8.cloned.1.call-start
  183.5 84.9 %reduce-scatter.5.cloned.1.call-done = f32[1,96,384]{2,1,0:T(8,128)} async-done(((f32[16,96,384]{2,1,0:T(8,128)}), f32[1,96,384]{2,1,0:T(8,128)}) %reduce-scatter.5.cloned.1.call-update) | async-done | bytes 147472 | tf_op jit(solution)/shard_map/reduce_scatter | solution.py:35
  268.4 1.7 add_divide_fusion
  270.1 67.9 %all-gather.8.cloned.1.call-done = f32[3072,384]{1,0:T(8,128)} async-done(((f32[96,384]{1,0:T(8,128)}), f32[3072,384]{1,0:T(8,128)}) %all-gather.8.cloned.1.call-update) | async-done | bytes 4718608 | tf_op jit(solution)/shard_map/all_gather | solution.py:74
  338.0 5.2 %fusion.2 = f32[96,384]{1,0:T(8,128)S(1)} fusion(f32[3072,384]{1,0:T(8,128)} %all-gather.8.cloned.1.call-done, f32[192,3072]{1,0:T(8,128)S(1)} %copy-done), kind=kOutput, calls=%fused_computation.3 | convolution fusion | flops 1358954496 | bytes 6045696 | tf_op jit(solution)/shard_map/dot_general | solution.py:45
  343.3 6.5 %fusion.10 = f32[96,3072]{1,0:T(8,128)S(1)} fusion(f32[96,384]{1,0:T(8,128)S(1)} %fusion.2, f32[3072,384]{1,0:T(8,128)} %all-gather.6.cloned.1.call-done), kind=kOutput, calls=%fused_computation.13 | convolution fusion | flops 1358954496 | bytes 6045696 | tf_op jit(solution)/shard_map/dot_general | solution.py:49
  349.8 0.1 copy.13
  349.8 41.5 %all_to_all.5 = f32[8,96,384]{2,1,0:T(8,128)S(1)} all-to-all(f32[8,96,384]{2,1,0:T(8,128)S(1)} %bitcast.25), channel_id=1, replica_groups=mesh['wide_0'=4,'wide_1'=4,'wide_2'=2,'narrow'=8] {'narrow'}, dimensions={0} | all-to-all | bytes 2359296 | tf_op jit(solution)/shard_map/all_to_all | solution.py:40
  391.3 0.7 reduce_sum.9
  (7 shorter events, 0.0 us)
Async XLA Ops:
  7.2 84.6 %all-gather.4.cloned.1.call-start = ((), (), s32[]{:S(2)}) async-start(), calls=%async_computation.3 | async-start | bytes 2654208 | tf_op jit(solution)/shard_map/all_gather | solution.py:20
  9.0 144.8 %all-gather.6.cloned.1.call-start = ((), (), s32[]{:S(2)}) async-start(), calls=%async_computation.4 | async-start | bytes 4866048 | tf_op jit(solution)/shard_map/all_gather | solution.py:60
  9.7 173.6 %reduce-scatter.3.cloned.1.call-start = ((), (), s32[]{:S(2)}) async-start(), calls=%async_computation.5 | async-start | bytes 7077888 | tf_op jit(solution)/shard_map/reduce_scatter | solution.py:34
  91.8 67.6 %copy-start = (f32[192,3072]{1,0:T(8,128)S(1)}, f32[192,3072]{1,0:T(8,128)}, u32[]{:S(2)}) copy-start(f32[192,3072]{1,0:T(8,128)} %all-gather.4.cloned.1.call-done) | copy-start | bytes 7077892
  165.9 102.5 %copy-start.1 = (f32[96,384]{1,0:T(8,128)S(1)}, f32[96,384]{1,0:T(8,128)}, u32[]{:S(2)}) copy-start(f32[96,384]{1,0:T(8,128)} %param.6) | copy-start | bytes 442372
  165.9 102.5 %copy-start.2 = (f32[96,384]{1,0:T(8,128)S(1)}, f32[96,384]{1,0:T(8,128)}, u32[]{:S(2)}) copy-start(f32[96,384]{1,0:T(8,128)} %param.7) | copy-start | bytes 442372
  165.9 102.5 %reduce-scatter.5.cloned.1.call-start = ((), (), s32[]{:S(2)}) async-start(), calls=%async_computation.6 | async-start | bytes 2506752 | tf_op jit(solution)/shard_map/reduce_scatter | solution.py:35
  183.3 154.7 %all-gather.8.cloned.1.call-start = ((), (), s32[]{:S(2)}) async-start(), calls=%async_computation.7 | async-start | bytes 4866048 | tf_op jit(solution)/shard_map/all_gather | solution.py:74
Sparse Core Ops, SparseCore 0:
  10.6 81.1 all-gather.3
  93.7 60.0 all-gather.5
  166.0 17.2 reduce-scatter.2
  185.9 82.5 reduce-scatter.4
  270.8 67.1 all-gather.7
where the time goes:
time: 399 us
  waiting for transfers between devices  315 us (79%)
  blocking collectives  41.5 us (10%)
  matrix products  21.2 us (5%)
  between operations  13.8 us (3%)
  other arithmetic  4.16 us (1%)
    reduce_scatter x1, waiting for transfers between devices, scatter_pairs(): return lax.psum_scatter(tiles, chips, scatter_dimension=0, tiled=True)[0]  84.9 us
    all_gather x1, waiting for transfers between devices, side_by_side(): lax.all_gather(both, axis, axis=dim, tiled=True)  82.1 us
    all_gather x1, waiting for transfers between devices, body(): lax.all_gather(direction, WIDE, axis=0, tiled=True)  67.9 us
    all_gather x1, waiting for transfers between devices, body(): right_panel = lax.all_gather(right_basis, WIDE, axis=0, tiled=True)  62 us
    all_to_all x1, blocking collectives, sent_and_summed(): lax.all_to_all(tiles, axis, split_axis=0, concat_axis=0, tiled=True)  41.5 us
    reduce_scatter x1, waiting for transfers between devices, scatter_pairs(): tiles = lax.psum_scatter(tiles, core, scatter_dimension=0, tiled=True)  17.3 us
    dot_general x2, matrix products, product(): jnp.dot(left, right, precision=lax.Precision.HIGHEST, preferred_element_t...  10.8 us
    dot_general x2, matrix products, contract(): lax.dot_general(left, right, (((left_dim,), (right_dim,)), ((), ())), pre...  10.4 us
  transfers between devices with their start and end apart: 5, of which 5 were waited for; matrix products, arithmetic and copies ran while one was open for 0% of the time, Pallas kernels for 0%

commit v1 on v0

--- a/solution.py
+++ b/solution.py
@@ -71,7 +71,12 @@
         / (jnp.sqrt(new_second / (1.0 - beta_second**STEP)) + epsilon)
     )
     columns = left_rows
-    back_left = product(columns, lax.all_gather(direction, WIDE, axis=0, tiled=True))
+    back_left = product(
+        columns,
+        jnp.concatenate(
+            lax.all_to_all(jnp.stack([direction] * lax.axis_size(WIDE)), WIDE, 0, 0), axis=0
+        ),
+    )
     terms = contract(back_left, right_panel, 1, 1)
     update = sent_and_summed(terms, "narrow", 1)
     return (update, new_first, new_second)

time: 399 us -> 444 us (1.11)
  blocking collectives: 41.5 us -> 158 us
  waiting for transfers between devices: 315 us -> 247 us
    all_to_all x0 -> x1, blocking collectives: none -> 116 us  [body(): lax.all_to_all(jnp.stack([direction] * lax.axis_size(WIDE)), WIDE, 0, 0)]
    all_gather x1 -> x0, waiting for transfers between devices: 67.9 us -> none  [body(): lax.all_gather(direction, WIDE, axis=0, tiled=True)]
  transfers between devices with their start and end apart: 5 -> 4, of which waited for: 5 -> 4; matrix products, arithmetic and copies ran while one was open for 0% -> 0% of each run, Pallas kernels for 0% -> 0%
where the time goes in v1:
time: 444 us
  waiting for transfers between devices  247 us (56%)
  blocking collectives  158 us (36%)
  matrix products  17.1 us (4%)
  between operations  13.9 us (3%)
    all_to_all x1, blocking collectives, body(): lax.all_to_all(jnp.stack([direction] * lax.axis_size(WIDE)), WIDE, 0, 0)  116 us
    reduce_scatter x1, waiting for transfers between devices, scatter_pairs(): return lax.psum_scatter(tiles, chips, scatter_dimension=0, tiled=True)[0]  85.1 us
    all_gather x1, waiting for transfers between devices, side_by_side(): lax.all_gather(both, axis, axis=dim, tiled=True)  82.1 us
    all_gather x1, waiting for transfers between devices, body(): right_panel = lax.all_gather(right_basis, WIDE, axis=0, tiled=True)  62 us
    all_to_all x1, blocking collectives, sent_and_summed(): lax.all_to_all(tiles, axis, split_axis=0, concat_axis=0, tiled=True)  42.3 us
    reduce_scatter x1, waiting for transfers between devices, scatter_pairs(): tiles = lax.psum_scatter(tiles, core, scatter_dimension=0, tiled=True)  17.3 us
  transfers between devices with their start and end apart: 4, of which 4 were waited for; matrix products, arithmetic and copies ran while one was open for 0% of the time, Pallas kernels for 0%

profile of v1, /device:TPU:32, one launch (start us, length us, event | category | flops | bytes accessed | tf_op | source)
XLA Modules:
  0.0 443.9 jit_solution(5256794154565857879)
XLA Ops:
  7.2 0.0 all-gather.3.cloned.1.call-start
  7.2 1.7 pad_maximum_fusion
  8.9 0.0 all-gather.3.cloned.1.call-update
  8.9 0.0 all-gather.5.cloned.1.call-start
  9.0 0.7 all-gather.5.cloned.1.call-update
  9.7 0.0 reduce-scatter.3.cloned.1.call-start
  9.7 82.1 %all-gather.3.cloned.1.call-done = f32[192,3072]{1,0:T(8,128)} async-done(((f32[192,384]{1,0:T(8,128)}), f32[192,3072]{1,0:T(8,128)}) %all-gather.3.cloned.1.call-update) | async-done | bytes 2359312 | tf_op jit(solution)/shard_map/all_gather | solution.py:20
  91.8 62.0 %all-gather.5.cloned.1.call-done = f32[3072,384]{1,0:T(8,128)} async-done(((f32[96,384]{1,0:T(8,128)}), f32[3072,384]{1,0:T(8,128)}) %all-gather.5.cloned.1.call-update) | async-done | bytes 4718608 | tf_op jit(solution)/shard_map/all_gather | solution.py:60
  153.8 5.6 %fusion = f32[96,384]{1,0:T(8,128)S(1)} fusion(f32[3072,384]{1,0:T(8,128)} %all-gather.5.cloned.1.call-done, f32[192,3072]{1,0:T(8,128)} %all-gather.3.cloned.1.call-done), kind=kOutput, calls=%fused_computation.1 | convolution fusion | flops 1358954496 | bytes 6045696 | tf_op jit(solution)/shard_map/dot_general | solution.py:45
  159.4 3.9 fusion.4
  163.3 2.5 copy.9
  165.9 0.0 reduce-scatter.3.cloned.1.call-update
  165.9 0.0 reduce-scatter.5.cloned.1.call-start
  166.0 17.3 %reduce-scatter.3.cloned.1.call-done = f32[16,96,384]{2,1,0:T(8,128)} async-done(((f32[32,96,384]{2,1,0:T(8,128)}), f32[16,96,384]{2,1,0:T(8,128)}) %reduce-scatter.3.cloned.1.call-update) | async-done | bytes 2359312 | tf_op jit(solution)/shard_map/reduce_scatter | solution.py:34
  183.3 0.0 reduce-scatter.5.cloned.1.call-update
  183.3 85.1 %reduce-scatter.5.cloned.1.call-done = f32[1,96,384]{2,1,0:T(8,128)} async-done(((f32[16,96,384]{2,1,0:T(8,128)}), f32[1,96,384]{2,1,0:T(8,128)}) %reduce-scatter.5.cloned.1.call-update) | async-done | bytes 147472 | tf_op jit(solution)/shard_map/reduce_scatter | solution.py:35
  268.4 1.7 add_divide_fusion
  270.1 0.5 stack.2
  270.7 116.1 %all_to_all.10 = f32[32,96,384]{2,1,0:T(8,128)S(1)} all-to-all(f32[32,96,384]{2,1,0:T(8,128)S(1)} %stack.2), channel_id=1, replica_groups=mesh['wide_0'=4,'wide_1'=4,'wide_2'=2,'narrow'=8] {'wide_0','wide_1','wi..., dimensions={0} | all-to-all | bytes 9437184 | tf_op jit(solution)/shard_map/all_to_all | solution.py:77
  386.7 2.9 fusion.2
  389.7 4.6 %fusion.10 = f32[96,3072]{1,0:T(8,128)S(1)} fusion(f32[96,384]{1,0:T(8,128)S(1)} %fusion.2, f32[3072,384]{1,0:T(8,128)S(1)} %bitcast.25), kind=kOutput, calls=%fused_computation.13 | convolution fusion | flops 1358954496 | bytes 6045696 | tf_op jit(solution)/shard_map/dot_general | solution.py:49
  394.3 0.1 copy.13
  394.4 42.3 %all_to_all.11 = f32[8,96,384]{2,1,0:T(8,128)S(1)} all-to-all(f32[8,96,384]{2,1,0:T(8,128)S(1)} %bitcast.29), channel_id=1, replica_groups=mesh['wide_0'=4,'wide_1'=4,'wide_2'=2,'narrow'=8] {'narrow'}, dimensions={0} | all-to-all | bytes 2359296 | tf_op jit(solution)/shard_map/all_to_all | solution.py:40
  436.7 0.7 reduce_sum.9
  (11 shorter events, 0.0 us)
Async XLA Ops:
  7.2 84.6 %all-gather.3.cloned.1.call-start = ((), (), s32[]{:S(2)}) async-start(), calls=%async_computation.4 | async-start | bytes 2654208 | tf_op jit(solution)/shard_map/all_gather | solution.py:20
  8.9 144.8 %all-gather.5.cloned.1.call-start = ((), (), s32[]{:S(2)}) async-start(), calls=%async_computation.5 | async-start | bytes 4866048 | tf_op jit(solution)/shard_map/all_gather | solution.py:60
  9.7 173.6 %reduce-scatter.3.cloned.1.call-start = ((), (), s32[]{:S(2)}) async-start(), calls=%async_computation.6 | async-start | bytes 7077888 | tf_op jit(solution)/shard_map/reduce_scatter | solution.py:34
  91.8 67.6 %copy-start = (f32[192,3072]{1,0:T(8,128)S(1)}, f32[192,3072]{1,0:T(8,128)}, u32[]{:S(2)}) copy-start(f32[192,3072]{1,0:T(8,128)} %all-gather.3.cloned.1.call-done) | copy-start | bytes 7077892
  165.9 102.5 %copy-start.1 = (f32[96,384]{1,0:T(8,128)S(1)}, f32[96,384]{1,0:T(8,128)}, u32[]{:S(2)}) copy-start(f32[96,384]{1,0:T(8,128)} %param.6) | copy-start | bytes 442372
  165.9 102.5 %copy-start.2 = (f32[96,384]{1,0:T(8,128)S(1)}, f32[96,384]{1,0:T(8,128)}, u32[]{:S(2)}) copy-start(f32[96,384]{1,0:T(8,128)} %param.7) | copy-start | bytes 442372
  165.9 102.5 %reduce-scatter.5.cloned.1.call-start = ((), (), s32[]{:S(2)}) async-start(), calls=%async_computation.7 | async-start | bytes 2506752 | tf_op jit(solution)/shard_map/reduce_scatter | solution.py:35
  270.1 119.6 %slice-start = ((s8[4718592]{0:T(1024)(128)(4,1)}), s8[4194304]{0:T(1024)(128)(4,1)S(1)}, s32[]{:S(2)}) async-start(s8[4718592]{0:T(1024)(128)(4,1)} %bitcast.24), calls=%async_computation.8 | async-start | bytes 8388608
  270.6 119.0 %slice-start.1 = ((s8[4718592]{0:T(1024)(128)(4,1)}), s8[524288]{0:T(1024)(128)(4,1)S(1)}, s32[]{:S(2)}) async-start(s8[4718592]{0:T(1024)(128)(4,1)} %bitcast.24), calls=%async_computation.9 | async-start | bytes 1048576
Sparse Core Ops, SparseCore 0:
  10.6 81.1 all-gather.2
  93.7 60.0 all-gather.4
  166.0 17.2 reduce-scatter.2
  185.8 82.5 reduce-scatter.4
